TPU v7x, 32 devices: a whole 2x2x4 slice. The times are simulated.
32 devices in a mesh: dp: 2 (over core), ctx: 4 (over z), tensor: 4 (over y, x).
Axes of the slice: x: 2, y: 2, z: 4, core: 2. Of those that a mesh axis runs over, the one named last changes fastest.
Arguments:
- tokens: bfloat16 [4096, 2048], P(('dp', 'ctx')), may hold values from -6 to 6
- lengths: int32 [2, 13], P('dp'), may hold values from 1 to 819, 2048 in all within a row
- parents: int32 [2, 13], P('dp'), may hold values from 0 to 4, as said below
- w_query: bfloat16 [2048, 2048], P(('dp', 'ctx'), 'tensor'), may hold values from -0.125 to 0.125
- w_key: bfloat16 [2048, 1024], P(('dp', 'ctx'), 'tensor'), may hold values from -0.125 to 0.125
- w_value: bfloat16 [2048, 1024], P(('dp', 'ctx'), 'tensor'), may hold values from -0.125 to 0.125
- w_out: bfloat16 [2048, 2048], P('tensor', ('dp', 'ctx')), may hold values from -1.5 to 1.5
- w_gate: bfloat16 [2048, 6144], P(('dp', 'ctx'), 'tensor'), may hold values from -0.125 to 0.125
- w_up: bfloat16 [2048, 6144], P(('dp', 'ctx'), 'tensor'), may hold values from -0.125 to 0.125
- w_down: bfloat16 [6144, 2048], P('tensor', ('dp', 'ctx')), may hold values from -0.078125 to 0.078125
- gain_attn: bfloat16 [2048], P(('dp', 'ctx')), may hold values from 0.099609375 to 1.8984375
- gain_mlp: bfloat16 [2048], P(('dp', 'ctx')), may hold values from 0.099609375 to 1.8984375
- gain_query: bfloat16 [128], P(('dp', 'ctx')), may hold values from 0.099609375 to 1.8984375
- gain_key: bfloat16 [128], P(('dp', 'ctx')), may hold values from 0.099609375 to 1.8984375
- cotangent: bfloat16 [4096, 2048], P(('dp', 'ctx')), may hold values from -6 to 6
Outputs:
- result: bfloat16 [4096, 2048], P(('dp', 'ctx'))
- grad_tokens: float32 [4096, 2048], P(('dp', 'ctx'))
- grad_query: float32 [2048, 2048], P(('dp', 'ctx'), 'tensor')
- grad_key: float32 [2048, 1024], P(('dp', 'ctx'), 'tensor')
- grad_value: float32 [2048, 1024], P(('dp', 'ctx'), 'tensor')
- grad_out: float32 [2048, 2048], P('tensor', ('dp', 'ctx'))
- grad_gate: float32 [2048, 6144], P(('dp', 'ctx'), 'tensor')
- grad_up: float32 [2048, 6144], P(('dp', 'ctx'), 'tensor')
- grad_down: float32 [6144, 2048], P('tensor', ('dp', 'ctx'))
- grad_gain_attn: float32 [2048], P(('dp', 'ctx'))
- grad_gain_mlp: float32 [2048], P(('dp', 'ctx'))
- grad_gain_query: float32 [128], P(('dp', 'ctx'))
- grad_gain_key: float32 [128], P(('dp', 'ctx'))
Inputs may be any that keep to these rules, and one draw needn't show every extreme that they name: lengths[t, s] counts the tokens of segment s of tree t; the segments lie in order and each tree's lengths sum to 2048. parents[t, s] is the segment from which segment s of tree t hangs; segments 0 to 4 name 0 (segment 0 is the root), segments 5 to 12 name one of 1 to 4.
All inputs are finite; a program needn't handle non-finite values.
Results may differ from a plain program's by a relative error of at most 0.02.
Values may be sent and summed in bfloat16 or wider, within the bound.
No kernel may reach another device: no remote copies, remote signals or barrier semaphores. Data moves between devices by JAX's collectives and lax.ppermute only.
A program may use at most 192 MiB of HBM per device.

v0:
```python
import math
import jax
import jax.numpy as jnp
from jax import lax
from jax.sharding import PartitionSpec as P

HEAD_DIM = 128
EPS = 1e-06
THETA = 1000000.0
PRECISE = lax.Precision.HIGHEST


def norm_rows(values, gain_vec):
    scales = lax.rsqrt(jnp.mean(values * values, axis=-1, keepdims=True) + EPS)
    return (values * scales * gain_vec, scales)


def norm_back(grad_in, values, gain_vec, scales):
    upstream = grad_in * gain_vec
    inner_mean = jnp.mean(upstream * values, axis=-1, keepdims=True)
    return (
        scales * upstream - values * scales * scales * scales * inner_mean,
        grad_in * values * scales,
    )


def rotate_pairs(values, cosine, sine_vals):
    half_dim = values.shape[-1] // 2
    first_half = values[..., :half_dim]
    second_half = values[..., half_dim:]
    return jnp.concatenate(
        [
            first_half * cosine - second_half * sine_vals,
            second_half * cosine + first_half * sine_vals,
        ],
        axis=-1,
    )


def rotate_back(values, cosine, sine_vals):
    half_dim = values.shape[-1] // 2
    first_half = values[..., :half_dim]
    second_half = values[..., half_dim:]
    return jnp.concatenate(
        [
            first_half * cosine + second_half * sine_vals,
            second_half * cosine - first_half * sine_vals,
        ],
        axis=-1,
    )


def inner_rows(left, right):
    return lax.dot_general(
        left, right, (((0,), (0,)), ((), ())), preferred_element_type=jnp.float32
    )


def outer_cols(left, right):
    return lax.dot_general(
        left, right, (((1,), (1,)), ((), ())), preferred_element_type=jnp.float32
    )


def tensor_sum(values):
    return lax.psum(values, "tensor")


def tree_layout(lengths, parents, tree_total):
    seg_count = lengths.shape[0]
    index = jnp.arange(seg_count, dtype=jnp.int32)
    direct = ((parents[:, None] == index[None, :]) & (parents[:, None] != index[:, None])).astype(
        jnp.float32
    )
    reach = direct
    for closure_step in range(4):
        reach = jnp.minimum(reach + jnp.dot(reach, reach, precision=PRECISE), 1.0)
    ends = jnp.cumsum(lengths, dtype=jnp.int32)
    starts = ends - lengths
    offset = jnp.dot(reach, lengths.astype(jnp.float32), precision=PRECISE)
    places = jnp.arange(tree_total, dtype=jnp.int32)
    member = (starts[None, :] <= places[:, None]).astype(jnp.int32)
    segment_ids = jnp.sum(member, axis=1, dtype=jnp.int32) - 1
    onehot = (segment_ids[:, None] == index[None, :]).astype(jnp.float32)
    base = jnp.dot(onehot, offset - starts.astype(jnp.float32), precision=PRECISE)
    position = places.astype(jnp.float32) + base
    return (segment_ids, onehot, reach, position)


def on_device(
    tokens,
    lengths,
    parents,
    w_query,
    w_key,
    w_value,
    w_out,
    w_gate,
    w_up,
    w_down,
    gain_attn,
    gain_mlp,
    gain_query,
    gain_key,
    cotangent,
):
    row_count = tokens.shape[0]
    tree_total = row_count * lax.axis_size("ctx")
    start_row = lax.axis_index("ctx") * row_count
    attn_set = (
        lax.all_gather(w_query, ("dp", "ctx"), axis=0, tiled=True),
        lax.all_gather(w_key, ("dp", "ctx"), axis=0, tiled=True),
        lax.all_gather(w_value, ("dp", "ctx"), axis=0, tiled=True),
        lax.all_gather(w_out, ("dp", "ctx"), axis=1, tiled=True),
        lax.all_gather(gain_attn, ("dp", "ctx"), axis=0, tiled=True),
        lax.all_gather(gain_query, ("dp", "ctx"), axis=0, tiled=True),
        lax.all_gather(gain_key, ("dp", "ctx"), axis=0, tiled=True),
    )
    mlp_set = (
        lax.all_gather(w_gate, ("dp", "ctx"), axis=0, tiled=True),
        lax.all_gather(w_up, ("dp", "ctx"), axis=0, tiled=True),
        lax.all_gather(w_down, ("dp", "ctx"), axis=1, tiled=True),
        lax.all_gather(gain_mlp, ("dp", "ctx"), axis=0, tiled=True),
    )
    wq_full, wk_full, wv_full, wo_full, gain_one, gain_q, gain_k = attn_set
    wg_full, wu_full, wd_full, gain_two = mlp_set
    segment_all, onehot_all, reach, position_all = tree_layout(lengths[0], parents[0], tree_total)
    segment_here = lax.dynamic_slice_in_dim(segment_all, start_row, row_count)
    onehot_here = lax.dynamic_slice_in_dim(onehot_all, start_row, row_count)
    position = lax.dynamic_slice_in_dim(position_all, start_row, row_count)
    place_here = start_row + jnp.arange(row_count, dtype=jnp.int32)
    place_all = jnp.arange(tree_total, dtype=jnp.int32)
    ancestor = (
        jnp.dot(jnp.dot(onehot_here, reach, precision=PRECISE), onehot_all.T, precision=PRECISE)
        > 0.5
    )
    allowed = (segment_here[:, None] == segment_all[None, :]) & (
        place_all[None, :] <= place_here[:, None]
    ) | ancestor
    half_dim = HEAD_DIM // 2
    frequency = jnp.exp(
        jnp.arange(half_dim, dtype=jnp.float32) * (-2.0 * math.log(THETA) / HEAD_DIM)
    )
    angles = position[:, None] * frequency[None, :]
    cosine = jnp.cos(angles)[:, None, :]
    sine_vals = jnp.sin(angles)[:, None, :]
    score_scale = 1.0 / math.sqrt(HEAD_DIM)
    inputs = tokens.astype(jnp.float32)
    gain_onef = gain_one.astype(jnp.float32)
    normed_f, scale_one = norm_rows(inputs, gain_onef)
    normed_attn = normed_f.astype(jnp.bfloat16)
    q_raw = jnp.dot(normed_attn, wq_full, preferred_element_type=jnp.float32)
    k_raw = jnp.dot(normed_attn, wk_full, preferred_element_type=jnp.float32)
    v_bf = jnp.dot(normed_attn, wv_full, preferred_element_type=jnp.float32).astype(jnp.bfloat16)
    heads_here = q_raw.shape[1] // HEAD_DIM
    kv_here = k_raw.shape[1] // HEAD_DIM
    group_size = heads_here // kv_here
    gain_qf = gain_q.astype(jnp.float32)
    gain_kf = gain_k.astype(jnp.float32)
    q_heads = q_raw.reshape(row_count, heads_here, HEAD_DIM)
    k_heads = k_raw.reshape(row_count, kv_here, HEAD_DIM)
    q_normed, q_scales = norm_rows(q_heads, gain_qf)
    k_normed, k_scales = norm_rows(k_heads, gain_kf)
    q_bf = rotate_pairs(q_normed, cosine, sine_vals).astype(jnp.bfloat16)
    k_bf = rotate_pairs(k_normed, cosine, sine_vals).astype(jnp.bfloat16)
    k_all, v_all = (
        lax.all_gather(k_bf.reshape(row_count, kv_here * HEAD_DIM), "ctx", axis=0, tiled=True),
        lax.all_gather(v_bf, "ctx", axis=0, tiled=True),
    )
    k_all = k_all.reshape(tree_total, kv_here, HEAD_DIM)
    v_all = v_all.reshape(tree_total, kv_here, HEAD_DIM)
    q_grouped = q_bf.reshape(row_count, kv_here, group_size, HEAD_DIM)
    scores = (
        jnp.einsum("tkgd,skd->kgts", q_grouped, k_all, preferred_element_type=jnp.float32)
        * score_scale
    )
    scores = jnp.where(allowed[None, None], scores, -1e30)
    row_max = jnp.max(scores, axis=-1, keepdims=True)
    weights = jnp.exp(scores - row_max)
    prob_all = weights / jnp.sum(weights, axis=-1, keepdims=True)
    prob_bf = prob_all.astype(jnp.bfloat16)
    mixture = jnp.einsum("kgts,skd->tkgd", prob_bf, v_all, preferred_element_type=jnp.float32)
    mixture_bf = mixture.reshape(row_count, heads_here * HEAD_DIM).astype(jnp.bfloat16)
    attn_term = jnp.dot(mixture_bf, wo_full, preferred_element_type=jnp.float32)
    gain_twof = gain_two.astype(jnp.float32)
    hidden = inputs + tensor_sum(attn_term)
    normed_g, scale_two = norm_rows(hidden, gain_twof)
    normed_mlp = normed_g.astype(jnp.bfloat16)
    gate_pre = jnp.dot(normed_mlp, wg_full, preferred_element_type=jnp.float32)
    up_pre = jnp.dot(normed_mlp, wu_full, preferred_element_type=jnp.float32)
    gate_sig = jax.nn.sigmoid(gate_pre)
    gate_act = gate_pre * gate_sig
    inner_bf = (gate_act * up_pre).astype(jnp.bfloat16)
    mlp_term = jnp.dot(inner_bf, wd_full, preferred_element_type=jnp.float32)
    result = (hidden + tensor_sum(mlp_term)).astype(jnp.bfloat16)
    grad_result = cotangent.astype(jnp.float32)
    grad_down = inner_rows(inner_bf, cotangent)
    grad_inner = outer_cols(cotangent, wd_full)
    grad_gate_pre = (grad_inner * up_pre * gate_sig * (1.0 + gate_pre * (1.0 - gate_sig))).astype(
        jnp.bfloat16
    )
    grad_up_pre = (grad_inner * gate_act).astype(jnp.bfloat16)
    grad_gate = inner_rows(normed_mlp, grad_gate_pre)
    grad_up = inner_rows(normed_mlp, grad_up_pre)
    mlp_back_term = outer_cols(grad_gate_pre, wg_full) + outer_cols(grad_up_pre, wu_full)
    grad_normed_mlp = tensor_sum(mlp_back_term)
    grad_hidden_norm, gain_two_terms = norm_back(grad_normed_mlp, hidden, gain_twof, scale_two)
    grad_gain_mlp = jnp.sum(gain_two_terms, axis=0)
    grad_hidden = grad_result + grad_hidden_norm
    grad_attn_bf = grad_hidden.astype(jnp.bfloat16)
    grad_out = inner_rows(mixture_bf, grad_attn_bf)
    grad_mixture = (
        outer_cols(grad_attn_bf, wo_full)
        .astype(jnp.bfloat16)
        .reshape(row_count, kv_here, group_size, HEAD_DIM)
    )
    grad_probs = jnp.einsum(
        "tkgd,skd->kgts", grad_mixture, v_all, preferred_element_type=jnp.float32
    )
    grad_v_all = jnp.einsum(
        "kgts,tkgd->skd", prob_bf, grad_mixture, preferred_element_type=jnp.float32
    )
    row_total = jnp.sum(prob_all * grad_probs, axis=-1, keepdims=True)
    grad_scores = (prob_all * (grad_probs - row_total)).astype(jnp.bfloat16)
    grad_q = (
        jnp.einsum("kgts,skd->tkgd", grad_scores, k_all, preferred_element_type=jnp.float32)
        * score_scale
    )
    grad_k_all = (
        jnp.einsum("kgts,tkgd->skd", grad_scores, q_grouped, preferred_element_type=jnp.float32)
        * score_scale
    )
    grad_k, grad_v = (
        lax.psum_scatter(
            grad_k_all.reshape(tree_total, kv_here * HEAD_DIM),
            "ctx",
            scatter_dimension=0,
            tiled=True,
        ),
        lax.psum_scatter(
            grad_v_all.reshape(tree_total, kv_here * HEAD_DIM),
            "ctx",
            scatter_dimension=0,
            tiled=True,
        ),
    )
    grad_q = (
        grad_q.reshape(row_count, heads_here, HEAD_DIM).astype(jnp.bfloat16).astype(jnp.float32)
    )
    grad_k = grad_k.reshape(row_count, kv_here, HEAD_DIM).astype(jnp.bfloat16).astype(jnp.float32)
    grad_v_bf = grad_v.astype(jnp.bfloat16)
    grad_q_heads, q_gain_terms = norm_back(
        rotate_back(grad_q, cosine, sine_vals), q_heads, gain_qf, q_scales
    )
    grad_k_heads, k_gain_terms = norm_back(
        rotate_back(grad_k, cosine, sine_vals), k_heads, gain_kf, k_scales
    )
    grad_q_raw = grad_q_heads.reshape(row_count, heads_here * HEAD_DIM).astype(jnp.bfloat16)
    grad_k_raw = grad_k_heads.reshape(row_count, kv_here * HEAD_DIM).astype(jnp.bfloat16)
    grad_query = inner_rows(normed_attn, grad_q_raw)
    grad_key = inner_rows(normed_attn, grad_k_raw)
    grad_value = inner_rows(normed_attn, grad_v_bf)
    partial_value = (
        outer_cols(grad_q_raw, wq_full)
        + outer_cols(grad_k_raw, wk_full)
        + outer_cols(grad_v_bf, wv_full)
    )
    q_gain_part = jnp.sum(q_gain_terms, axis=(0, 1))
    k_gain_part = jnp.sum(k_gain_terms, axis=(0, 1))
    grad_normed_attn, grad_gain_query, grad_gain_key = (
        lax.psum(partial_value.astype(jnp.bfloat16), "tensor").astype(jnp.float32),
        lax.psum(q_gain_part.astype(jnp.bfloat16), "tensor").astype(jnp.float32),
        lax.psum(k_gain_part.astype(jnp.bfloat16), "tensor").astype(jnp.float32),
    )
    grad_input_norm, gain_one_terms = norm_back(grad_normed_attn, inputs, gain_onef, scale_one)
    grad_tokens = grad_hidden + grad_input_norm
    grad_gain_attn = jnp.sum(gain_one_terms, axis=0)
    (
        grad_query,
        grad_key,
        grad_value,
        grad_out,
        grad_gate,
        grad_up,
        grad_down,
        grad_gain_attn,
        grad_gain_mlp,
        grad_gain_query,
        grad_gain_key,
    ) = (
        lax.psum_scatter(
            grad_query.astype(jnp.bfloat16), ("dp", "ctx"), scatter_dimension=0, tiled=True
        ).astype(jnp.float32),
        lax.psum_scatter(
            grad_key.astype(jnp.bfloat16), ("dp", "ctx"), scatter_dimension=0, tiled=True
        ).astype(jnp.float32),
        lax.psum_scatter(
            grad_value.astype(jnp.bfloat16), ("dp", "ctx"), scatter_dimension=0, tiled=True
        ).astype(jnp.float32),
        lax.psum_scatter(
            grad_out.astype(jnp.bfloat16), ("dp", "ctx"), scatter_dimension=1, tiled=True
        ).astype(jnp.float32),
        lax.psum_scatter(
            grad_gate.astype(jnp.bfloat16), ("dp", "ctx"), scatter_dimension=0, tiled=True
        ).astype(jnp.float32),
        lax.psum_scatter(
            grad_up.astype(jnp.bfloat16), ("dp", "ctx"), scatter_dimension=0, tiled=True
        ).astype(jnp.float32),
        lax.psum_scatter(
            grad_down.astype(jnp.bfloat16), ("dp", "ctx"), scatter_dimension=1, tiled=True
        ).astype(jnp.float32),
        lax.psum_scatter(
            grad_gain_attn.astype(jnp.bfloat16), ("dp", "ctx"), scatter_dimension=0, tiled=True
        ).astype(jnp.float32),
        lax.psum_scatter(
            grad_gain_mlp.astype(jnp.bfloat16), ("dp", "ctx"), scatter_dimension=0, tiled=True
        ).astype(jnp.float32),
        lax.psum_scatter(
            grad_gain_query.astype(jnp.bfloat16), ("dp", "ctx"), scatter_dimension=0, tiled=True
        ).astype(jnp.float32),
        lax.psum_scatter(
            grad_gain_key.astype(jnp.bfloat16), ("dp", "ctx"), scatter_dimension=0, tiled=True
        ).astype(jnp.float32),
    )
    return (
        result,
        grad_tokens,
        grad_query,
        grad_key,
        grad_value,
        grad_out,
        grad_gate,
        grad_up,
        grad_down,
        grad_gain_attn,
        grad_gain_mlp,
        grad_gain_query,
        grad_gain_key,
    )


def solution(mesh):
    placed = (
        P(("dp", "ctx"), None),
        P("dp", None),
        P("dp", None),
        P(("dp", "ctx"), "tensor"),
        P(("dp", "ctx"), "tensor"),
        P(("dp", "ctx"), "tensor"),
        P("tensor", ("dp", "ctx")),
        P(("dp", "ctx"), "tensor"),
        P(("dp", "ctx"), "tensor"),
        P("tensor", ("dp", "ctx")),
        P(("dp", "ctx")),
        P(("dp", "ctx")),
        P(("dp", "ctx")),
        P(("dp", "ctx")),
        P(("dp", "ctx"), None),
    )
    return jax.shard_map(
        on_device,
        mesh=mesh,
        in_specs=placed,
        out_specs=(
            P(("dp", "ctx"), None),
            P(("dp", "ctx"), None),
            P(("dp", "ctx"), "tensor"),
            P(("dp", "ctx"), "tensor"),
            P(("dp", "ctx"), "tensor"),
            P("tensor", ("dp", "ctx")),
            P(("dp", "ctx"), "tensor"),
            P(("dp", "ctx"), "tensor"),
            P("tensor", ("dp", "ctx")),
            P(("dp", "ctx")),
            P(("dp", "ctx")),
            P(("dp", "ctx")),
            P(("dp", "ctx")),
        ),
        check_vma=False,
    )
```

profile of v0, /device:TPU:0, one launch (start us, length us, event | category | flops | bytes accessed | tf_op | source)
XLA Modules:
  0.0 1460.9 jit_solution(8026323037325675424)
XLA Ops:
  9.4 17.9 %all-gather = bf16[8,1,256]{2,1,0:T(2,128)(2,1)S(1)} all-gather(bf16[1,1,256]{2,1,0:T(2,128)(2,1)S(1)} %reshape.243), channel_id=1, replica_groups=mesh['dp'=2,'ctx'=4,'tensor'=4] {'dp','ctx'}, dimensions={0}, use_global_device_ids=true | all-gather | bytes 4608 | tf_op jit(solution)/shard_map/all_gather | solution.py:115
  29.6 4.9 all-gather.12.cloned.1.call-done
  34.6 3.3 convolution_convert_fusion.8
  40.3 16.3 %all-reduce.8 = (bf16[128]{0:T(256)(128)(2,1)S(1)}, bf16[128]{0:T(256)(128)(2,1)S(1)}) all-reduce(bf16[128]{0:T(256)(128)(2,1)S(1)} %dynamic-update-slice, bf16[128]{0:T(256)(128)(2,1)S(1)} %dynamic-update-slice.1), channel_id=1, replica_groups=mesh['dp'=2,'ctx'=4,'tensor'=4] {'dp','ctx'}, use_global_device_ids=true, to_apply=%add | all-reduce | flops 256 | bytes 1024
  64.4 3.2 fusion.25
  70.3 17.6 %all-gather.14.cloned.1.call-done = bf16[2048,256]{1,0:T(8,128)(2,1)} async-done(((bf16[512,256]{1,0:T(8,128)(2,1)}), bf16[2048,256]{1,0:T(8,128)(2,1)}) %all-gather.14.cloned.1.call-update) | async-done | bytes 1048592 | tf_op jit(solution)/shard_map/all_gather | solution.py:168
  90.2 27.7 %all-gather.20.cloned.1.call-done = bf16[2048,512]{1,0:T(8,128)(2,1)} async-done(((bf16[256,512]{1,0:T(8,128)(2,1)}), bf16[2048,512]{1,0:T(8,128)(2,1)}) %all-gather.20.cloned.1.call-update) | async-done | bytes 2097168 | tf_op jit(solution)/shard_map/all_gather | solution.py:111
  122.8 24.4 %all-gather.18.cloned.1.call-done = bf16[2048,256]{0,1:T(8,128)(2,1)} async-done(((bf16[512,256]{0,1:T(8,128)(2,1)}), bf16[2048,256]{0,1:T(8,128)(2,1)}) %all-gather.18.cloned.1.call-update) | async-done | bytes 1048592 | tf_op jit(solution)/shard_map/all_gather | solution.py:167
  147.3 13.9 fusion.81
  161.2 7.6 fusion.32
  168.8 9.9 all-gather.22.cloned.1.call-done
  178.7 4.9 fusion.82
  185.8 16.4 %all-gather.1 = bf16[8,1,256]{2,1,0:T(2,128)(2,1)S(1)} all-gather(bf16[1,1,256]{2,1,0:T(2,128)(2,1)S(1)} %reshape.245), channel_id=1, replica_groups=mesh['dp'=2,'ctx'=4,'tensor'=4] {'dp','ctx'}, dimensions={0}, use_global_device_ids=true | all-gather | bytes 4608 | tf_op jit(solution)/shard_map/all_gather | solution.py:123
  202.2 84.2 %all-reduce.14.cloned.1.call-done = f32[512,2048]{1,0:T(8,128)} async-done(((f32[512,2048]{1,0:T(8,128)}), f32[512,2048]{1,0:T(8,128)}) %all-reduce.14.cloned.1.call-update) | async-done | bytes 4194320 | tf_op jit(solution)/shard_map/psum | solution.py:66
  293.0 59.8 %all-gather.24.cloned.1.call-done = bf16[2048,1536]{1,0:T(8,128)(2,1)} async-done(((bf16[256,1536]{1,0:T(8,128)(2,1)}), bf16[2048,1536]{1,0:T(8,128)(2,1)}) %all-gather.24.cloned.1.call-update) | async-done | bytes 6291472 | tf_op jit(solution)/shard_map/all_gather | solution.py:120
  352.8 8.5 fusion.83
  361.3 56.5 %all-gather.26.cloned.1.call-done = bf16[2048,1536]{1,0:T(8,128)(2,1)} async-done(((bf16[256,1536]{1,0:T(8,128)(2,1)}), bf16[2048,1536]{1,0:T(8,128)(2,1)}) %all-gather.26.cloned.1.call-update) | async-done | bytes 6291472 | tf_op jit(solution)/shard_map/all_gather | solution.py:121
  417.7 8.5 fusion.84
  426.2 56.8 %all-gather.28.cloned.1.call-done = bf16[1536,2048]{1,0:T(8,128)(2,1)} async-done(((bf16[1536,256]{1,0:T(8,128)(2,1)}), bf16[1536,2048]{1,0:T(8,128)(2,1)}) %all-gather.28.cloned.1.call-update) | async-done | bytes 6291472 | tf_op jit(solution)/shard_map/all_gather | solution.py:122
  483.0 9.8 multiply_convert_fusion.1
  492.9 7.3 fusion.86
  500.2 4.9 fusion.85
  505.2 5.0 convolution_add_fusion
  510.3 170.3 %all-reduce.18.cloned.1.call-done = (f32[512,2048]{1,0:T(8,128)}, f32[512,2048]{1,0:T(8,128)}) async-done(((f32[512,2048]{1,0:T(8,128)}, f32[512,2048]{1,0:T(8,128)}), (f32[512,2048]{1,0:T(8,128)}, f32[512,2048]{1,0:T(8,128)})) %all-reduce.18.cloned.1.call-update) | async-done | bytes 8388624 | tf_op jit(solution)/shard_map/psum | solution.py:66
  680.6 4.7 multiply_reduce_fusion
  685.3 6.6 subtract_add_fusion
  696.3 9.5 fusion.1
  705.7 11.6 fusion.3
  717.3 3.9 fusion.27
  721.4 10.0 fusion.20
  731.7 5.1 fusion.31
  740.9 4.8 convolution_convert_fusion.3
  745.8 8.2 convolution_convert_fusion.2
  754.1 8.2 convolution_convert_fusion.1
  770.1 40.8 %reduce-scatter.12.cloned.1.call-done = f32[512,256]{0,1:T(8,128)} async-done(((f32[2048,256]{0,1:T(8,128)}), f32[512,256]{0,1:T(8,128)}) %reduce-scatter.12.cloned.1.call-update) | async-done | bytes 524304 | tf_op jit(solution)/shard_map/reduce_scatter | solution.py:240
  813.6 4.3 add_convert_fusion
  818.0 8.2 convolution_convert_fusion
  831.6 29.7 %reduce-scatter.14.cloned.1.call-done = bf16[256,512]{1,0:T(8,128)(2,1)} async-done(((bf16[2048,512]{1,0:T(8,128)(2,1)}), bf16[256,512]{1,0:T(8,128)(2,1)}) %reduce-scatter.14.cloned.1.call-update) | async-done | bytes 262160 | tf_op jit(solution)/shard_map/reduce_scatter | solution.py:291
  863.2 48.6 %reduce-scatter.20.cloned.1.call-done = bf16[512,256]{1,0:T(8,128)(2,1)} async-done(((bf16[512,2048]{1,0:T(8,128)(2,1)}), bf16[512,256]{1,0:T(8,128)(2,1)}) %reduce-scatter.20.cloned.1.call-update) | async-done | bytes 262160 | tf_op jit(solution)/shard_map/reduce_scatter | solution.py:300
  913.6 127.4 %reduce-scatter.22.cloned.1.call-done = bf16[256,1536]{1,0:T(8,128)(2,1)} async-done(((bf16[2048,1536]{1,0:T(8,128)(2,1)}), bf16[256,1536]{1,0:T(8,128)(2,1)}) %reduce-scatter.22.cloned.1.call-update) | async-done | bytes 786448 | tf_op jit(solution)/shard_map/reduce_scatter | solution.py:303
  1043.4 128.1 %reduce-scatter.24.cloned.1.call-done = bf16[256,1536]{1,0:T(8,128)(2,1)} async-done(((bf16[2048,1536]{1,0:T(8,128)(2,1)}), bf16[256,1536]{1,0:T(8,128)(2,1)}) %reduce-scatter.24.cloned.1.call-update) | async-done | bytes 786448 | tf_op jit(solution)/shard_map/reduce_scatter | solution.py:306
  1174.0 70.6 %all-reduce.16.cloned.1.call-done = bf16[512,2048]{1,0:T(8,128)(2,1)} async-done(((bf16[512,2048]{1,0:T(8,128)(2,1)}), bf16[512,2048]{1,0:T(8,128)(2,1)}) %all-reduce.16.cloned.1.call-update) | async-done | bytes 2097168 | tf_op jit(solution)/shard_map/psum | solution.py:271
  1247.7 20.1 %all-reduce.7 = (bf16[2048]{0:T(1024)(128)(2,1)S(1)}, bf16[2048]{0:T(1024)(128)(2,1)S(1)}, bf16[128]{0:T(256)(128)(2,1)S(1)}, bf16[128]{0:T(256)(128)(2,1)S(1)}) all-reduce(bf16[2048]{0:T(1024)(128)(2,1)S(1)} %get-tuple-element.15, ...), channel_id=11, replica_groups=mesh['dp'=2,'ctx'=4,'tensor'=4] {'dp','ctx'}, use_global_device_ids=true, to_apply=%region_27.28.clone | all-reduce | flops 4352 | bytes 17408
  1268.0 108.0 %reduce-scatter.26.cloned.1.call-done = bf16[1536,256]{1,0:T(8,128)(2,1)} async-done(((bf16[1536,2048]{1,0:T(8,128)(2,1)}), bf16[1536,256]{1,0:T(8,128)(2,1)}) %reduce-scatter.26.cloned.1.call-update) | async-done | bytes 786448 | tf_op jit(solution)/shard_map/reduce_scatter | solution.py:309
  1378.4 9.8 all-reduce.9
  1389.2 25.4 %reduce-scatter.16.cloned.1.call-done = bf16[256,256]{1,0:T(8,128)(2,1)} async-done(((bf16[2048,256]{1,0:T(8,128)(2,1)}), bf16[256,256]{1,0:T(8,128)(2,1)}) %reduce-scatter.16.cloned.1.call-update) | async-done | bytes 131088 | tf_op jit(solution)/shard_map/reduce_scatter | solution.py:294
  1416.8 6.3 fusion.15
  1423.2 28.8 %reduce-scatter.18.cloned.1.call-done = bf16[256,256]{1,0:T(8,128)(2,1)} async-done(((bf16[2048,256]{1,0:T(8,128)(2,1)}), bf16[256,256]{1,0:T(8,128)(2,1)}) %reduce-scatter.18.cloned.1.call-update) | async-done | bytes 131088 | tf_op jit(solution)/shard_map/reduce_scatter | solution.py:297
  (231 shorter events, 75.0 us)
Async XLA Ops:
  7.2 27.4 %all-gather.12.cloned.1.call-start = ((), (), s32[]{:S(2)}) async-start(), calls=%async_computation.9 | async-start | bytes 1179648 | tf_op jit(solution)/shard_map/all_gather | solution.py:113
  7.9 51.2 %all-gather.16.cloned.1.call-start = ((), (), s32[]{:S(2)}) async-start(), calls=%async_computation.11 | async-start | bytes 1179648 | tf_op jit(solution)/shard_map/all_gather | solution.py:112
  8.7 79.2 %all-gather.14.cloned.1.call-start = ((), (), s32[]{:S(2)}) async-start(), calls=%async_computation.10 | async-start | bytes 1310720 | tf_op jit(solution)/shard_map/all_gather | solution.py:168
  27.3 90.6 %copy-start.21 = (f32[8,1,256]{2,1,0:T(1,128)}, f32[8,1,256]{2,1,0:T(1,128)S(1)}, u32[]{:S(2)}) copy-start(f32[8,1,256]{2,1,0:T(1,128)S(1)} %convert_element_type.255) | copy-start | bytes 24580
  27.3 11.3 copy-start.33
  27.3 12.5 copy-start.35
  27.3 12.8 copy-start.36
  27.3 29.3 %copy-start.34 = (s32[1,13]{1,0:T(1,128)S(1)}, s32[1,13]{1,0:T(1,128)}, u32[]{:S(2)}) copy-start(s32[1,13]{1,0:T(1,128)} %param.16) | copy-start | bytes 160
  27.3 29.5 %copy-start.37 = (s32[1,13]{1,0:T(1,128)S(1)}, s32[1,13]{1,0:T(1,128)}, u32[]{:S(2)}) copy-start(s32[1,13]{1,0:T(1,128)} %param.17) | copy-start | bytes 160
  27.4 31.8 %copy-start.3 = (bf16[512,2048]{1,0:T(8,128)(2,1)S(1)}, bf16[512,2048]{1,0:T(8,128)(2,1)}, u32[]{:S(2)}) copy-start(bf16[512,2048]{1,0:T(8,128)(2,1)} %param.15) | copy-start | bytes 6291460
  29.6 88.3 %copy-start.27 = (f32[512]{0:T(512)}, f32[512]{0:T(512)S(1)}, u32[]{:S(2)}) copy-start(f32[512]{0:T(512)S(1)} %add_rsqrt_fusion.3) | copy-start | bytes 6148
  37.9 80.0 %all-gather.20.cloned.1.call-start = ((), (), s32[]{:S(2)}) async-start(), calls=%async_computation.13 | async-start | bytes 2359296 | tf_op jit(solution)/shard_map/all_gather | solution.py:111
  38.5 108.8 %all-gather.18.cloned.1.call-start = ((), (), s32[]{:S(2)}) async-start(), calls=%async_computation.12 | async-start | bytes 1310720 | tf_op jit(solution)/shard_map/all_gather | solution.py:167
  59.1 63.0 %copy-start.10 = (f32[512,64]{0,1:T(8,128)}, f32[512,64]{0,1:T(8,128)S(1)}, u32[]{:S(2)}) copy-start(f32[512,64]{0,1:T(8,128)S(1)} %get-tuple-element.50) | copy-start | bytes 393220
  59.1 63.0 %copy-start.12 = (f32[512,64]{0,1:T(8,128)}, f32[512,64]{0,1:T(8,128)S(1)}, u32[]{:S(2)}) copy-start(f32[512,64]{0,1:T(8,128)S(1)} %get-tuple-element.51) | copy-start | bytes 393220
  63.1 115.6 %all-gather.22.cloned.1.call-start = ((), (), s32[]{:S(2)}) async-start(), calls=%async_computation.14 | async-start | bytes 2359296 | tf_op jit(solution)/shard_map/all_gather | solution.py:114
  63.7 222.7 %all-reduce.14.cloned.1.call-start = ((), (), s32[]{:S(2)}) async-start(), calls=%async_computation.15 | async-start | bytes 8388608 | tf_op jit(solution)/shard_map/psum | solution.py:66
  64.2 56.7 %copy-start.29 = (f32[128]{0:T(128)}, f32[128]{0:T(128)S(1)}, u32[]{:S(2)}) copy-start(f32[128]{0:T(128)S(1)} %convert_element_type.203) | copy-start | bytes 1540
  122.8 38.3 %copy-start.14 = (bf16[512,4,64]{2,0,1:T(8,128)(2,1)}, bf16[512,4,64]{2,0,1:T(8,128)(2,1)S(1)}, u32[]{:S(2)}) copy-start(bf16[512,4,64]{2,0,1:T(8,128)(2,1)S(1)} %copy.66) | copy-start | bytes 786436
  168.8 14.8 %copy-start.18 = (bf16[2,128,2,512]{3,1,2,0:T(8,128)(2,1)}, bf16[2,128,2,512]{3,1,2,0:T(8,128)(2,1)S(1)}, u32[]{:S(2)}) copy-start(bf16[2,128,2,512]{3,1,2,0:T(8,128)(2,1)S(1)} %fusion.32) | copy-start | bytes 1572868
  183.7 169.1 %all-gather.24.cloned.1.call-start = ((), (), s32[]{:S(2)}) async-start(), calls=%async_computation.16 | async-start | bytes 7077888 | tf_op jit(solution)/shard_map/all_gather | solution.py:120
  184.4 233.3 %all-gather.26.cloned.1.call-start = ((), (), s32[]{:S(2)}) async-start(), calls=%async_computation.17 | async-start | bytes 7077888 | tf_op jit(solution)/shard_map/all_gather | solution.py:121
  185.1 297.8 %all-gather.28.cloned.1.call-start = ((), (), s32[]{:S(2)}) async-start(), calls=%async_computation.18 | async-start | bytes 7077888 | tf_op jit(solution)/shard_map/all_gather | solution.py:122
  185.7 494.9 %all-reduce.18.cloned.1.call-start = ((), (), s32[]{:S(2)}) async-start(), calls=%async_computation.29 | async-start | bytes 16777216 | tf_op jit(solution)/shard_map/psum | solution.py:66
  483.0 17.2 %slice-start.6 = ((s8[6291456]{0:T(1024)(128)(4,1)}), s8[4194304]{0:T(1024)(128)(4,1)S(1)}, s32[]{:S(2)}) async-start(s8[6291456]{0:T(1024)(128)(4,1)} %bitcast.248), calls=%async_computation.36 | async-start | bytes 8388608
  483.0 22.2 %slice-start.4 = ((s8[6291456]{0:T(1024)(128)(4,1)}), s8[2097152]{0:T(1024)(128)(4,1)S(1)}, s32[]{:S(2)}) async-start(s8[6291456]{0:T(1024)(128)(4,1)} %bitcast.246), calls=%async_computation.34 | async-start | bytes 4194304
  492.8 7.3 copy-start.42
  492.8 7.3 copy-start.41
  492.9 12.3 copy-start.40
  492.9 7.3 slice-start.7
  492.9 12.3 slice-start.5
  510.2 255.5 %reduce-scatter.10.cloned.1.call-start = ((), (), s32[]{:S(2)}) async-start(), calls=%async_computation.19 | async-start | bytes 2621440 | tf_op jit(solution)/shard_map/reduce_scatter | solution.py:234
  680.6 15.6 %slice-start = ((s8[16777216]{0:T(1024)(128)(4,1)}), s8[4194304]{0:T(1024)(128)(4,1)S(1)}, s32[]{:S(2)}) async-start(s8[16777216]{0:T(1024)(128)(4,1)} %bitcast.216), calls=%async_computation.30 | async-start | bytes 8388608
  685.3 8.8 copy-start.16
  685.3 10.8 slice-start.1
  685.3 10.8 slice-start.2
  685.3 11.0 slice-start.3
  705.7 11.6 copy-start.15
  721.3 10.4 copy-start.30
  721.3 89.6 %reduce-scatter.12.cloned.1.call-start = ((), (), s32[]{:S(2)}) async-start(), calls=%async_computation.20 | async-start | bytes 2621440 | tf_op jit(solution)/shard_map/reduce_scatter | solution.py:240
  731.4 130.0 %reduce-scatter.14.cloned.1.call-start = ((), (), s32[]{:S(2)}) async-start(), calls=%async_computation.22 | async-start | bytes 2359296 | tf_op jit(solution)/shard_map/reduce_scatter | solution.py:291
  740.9 170.9 %reduce-scatter.20.cloned.1.call-start = ((), (), s32[]{:S(2)}) async-start(), calls=%async_computation.25 | async-start | bytes 2359296 | tf_op jit(solution)/shard_map/reduce_scatter | solution.py:300
  745.8 295.2 %reduce-scatter.22.cloned.1.call-start = ((), (), s32[]{:S(2)}) async-start(), calls=%async_computation.26 | async-start | bytes 7077888 | tf_op jit(solution)/shard_map/reduce_scatter | solution.py:303
  754.1 417.5 %reduce-scatter.24.cloned.1.call-start = ((), (), s32[]{:S(2)}) async-start(), calls=%async_computation.27 | async-start | bytes 7077888 | tf_op jit(solution)/shard_map/reduce_scatter | solution.py:306
  762.3 482.3 %all-reduce.16.cloned.1.call-start = ((), (), s32[]{:S(2)}) async-start(), calls=%async_computation.21 | async-start | bytes 4194304 | tf_op jit(solution)/shard_map/psum | solution.py:271
  817.9 558.1 %reduce-scatter.26.cloned.1.call-start = ((), (), s32[]{:S(2)}) async-start(), calls=%async_computation.28 | async-start | bytes 7077888 | tf_op jit(solution)/shard_map/reduce_scatter | solution.py:309
  826.2 588.4 %reduce-scatter.16.cloned.1.call-start = ((), (), s32[]{:S(2)}) async-start(), calls=%async_computation.23 | async-start | bytes 1179648 | tf_op jit(solution)/shard_map/reduce_scatter | solution.py:294
  828.2 623.7 %reduce-scatter.18.cloned.1.call-start = ((), (), s32[]{:S(2)}) async-start(), calls=%async_computation.24 | async-start | bytes 1179648 | tf_op jit(solution)/shard_map/reduce_scatter | solution.py:297
  (24 other events, 69.1 us)
Sparse Core Ops, SparseCore 0:
  9.6 24.9 all-gather.11
  36.2 22.2 all-gather.15
  60.6 27.1 all-gather.13
  89.3 28.5 all-gather.19
  119.9 27.3 all-gather.17
  148.7 29.9 all-gather.21
  183.8 102.6 all-reduce.13
  288.0 64.6 all-gather.23
  354.4 63.3 all-gather.25
  419.2 63.7 all-gather.27
  510.3 170.2 all-reduce.17
  721.4 44.2 reduce-scatter.9
  768.0 42.8 reduce-scatter.11
  813.0 48.2 reduce-scatter.13
  863.5 48.2 reduce-scatter.19
  914.0 126.9 reduce-scatter.21
  1043.1 128.3 reduce-scatter.23
  1174.5 70.0 all-reduce.15
  1246.9 129.0 reduce-scatter.25
  1378.1 36.3 reduce-scatter.15
  1416.8 35.0 reduce-scatter.17
where the time goes:
time: 1470 us; the launch traced here: 1460 us
  waiting for transfers between devices  1130 us (77%)
  matrix products  160 us (11%)
  blocking collectives  80.5 us (5%)
  other arithmetic  60.2 us (4%)
  between operations  17.6 us (1%)
    psum x2, waiting for transfers between devices, tensor_sum(): return lax.psum(values, 'tensor')  255 us
    reduce_scatter x1, waiting for transfers between devices, on_device(): lax.psum_scatter(grad_up.astype(jnp.bfloat16), ('dp', 'ctx'), scatter_dim...  128 us
    reduce_scatter x1, waiting for transfers between devices, on_device(): lax.psum_scatter(grad_gate.astype(jnp.bfloat16), ('dp', 'ctx'), scatter_d...  127 us
    reduce_scatter x1, waiting for transfers between devices, on_device(): lax.psum_scatter(grad_down.astype(jnp.bfloat16), ('dp', 'ctx'), scatter_d...  108 us
    psum x1, waiting for transfers between devices, on_device(): lax.psum(partial_value.astype(jnp.bfloat16), 'tensor').astype(jnp.float32)  70.6 us
    all_gather x1, waiting for transfers between devices, on_device(): lax.all_gather(w_gate, ('dp', 'ctx'), axis=0, tiled=True)  59.8 us
    all_gather x1, waiting for transfers between devices, on_device(): lax.all_gather(w_down, ('dp', 'ctx'), axis=1, tiled=True)  56.8 us
    all_gather x1, waiting for transfers between devices, on_device(): lax.all_gather(w_up, ('dp', 'ctx'), axis=0, tiled=True)  56.5 us
  transfers between devices with their start and end apart: 21, of which 20 were waited for; matrix products, arithmetic and copies ran while one was open for 11% of the time, Pallas kernels for 0%

commit v1 on v0

--- a/solution.py
+++ b/solution.py
@@ -8,6 +8,28 @@
 EPS = 1e-06
 THETA = 1000000.0
 PRECISE = lax.Precision.HIGHEST
+
+
+def in_order(parts, dim):
+    parts = jnp.moveaxis(parts, 0, dim)
+    shape = parts.shape
+    return parts.reshape(*shape[:dim], shape[dim] * shape[dim + 1], *shape[dim + 2 :])
+
+
+def gather_around(value, axis, dim):
+    size = lax.axis_size(axis)
+    pairs = [(i, (i + 1) % size) for i in range(size)]
+    back = [(b, a) for a, b in pairs]
+    lower, upper = ([], [])
+    for turn in range(size - 1):
+        if turn % 2 == 0:
+            lower.append(lax.ppermute(lower[-1] if lower else value, axis, pairs))
+        else:
+            upper.append(lax.ppermute(upper[-1] if upper else value, axis, back))
+    blocks = jnp.stack([*lower[::-1], value, *upper])
+    shift = lax.axis_index(axis) - len(lower)
+    blocks = blocks[(jnp.arange(size) - shift) % size]
+    return in_order(blocks, dim)
 
 
 def norm_rows(values, gain_vec):
@@ -117,7 +139,7 @@
         lax.all_gather(gain_key, ("dp", "ctx"), axis=0, tiled=True),
     )
     mlp_set = (
-        lax.all_gather(w_gate, ("dp", "ctx"), axis=0, tiled=True),
+        gather_around(w_gate, ("dp", "ctx"), 0),
         lax.all_gather(w_up, ("dp", "ctx"), axis=0, tiled=True),
         lax.all_gather(w_down, ("dp", "ctx"), axis=1, tiled=True),
         lax.all_gather(gain_mlp, ("dp", "ctx"), axis=0, tiled=True),

time: 1470 us -> 1420 us (0.966)
  waiting for transfers between devices: 1130 us -> 1030 us
  blocking collectives: 80.5 us -> 105 us
  local copies, waits for them, and re-layouts: 14.5 us -> 34.4 us
    ppermute x0 -> x7, waiting for transfers between devices: none -> 108 us  [the longest x3 57.4 us: gather_around(): upper.append(lax.ppermute(upper[-1] if upper else value, axis, back))]
    psum x2, waiting for transfers between devices: 255 us -> 170 us  [tensor_sum(): return lax.psum(values, 'tensor')]
    all_gather x1 -> x0, waiting for transfers between devices: 59.8 us -> none  [on_device(): lax.all_gather(w_gate, ('dp', 'ctx'), axis=0, tiled=True)]
    all_gather x1, waiting for transfers between devices: 56.5 us -> 0.01 us  [on_device(): lax.all_gather(w_up, ('dp', 'ctx'), axis=0, tiled=True)]
    all_gather x1, blocking collectives: 16.4 us -> 41.2 us  [on_device(): lax.all_gather(gain_mlp, ('dp', 'ctx'), axis=0, tiled=True)]
  transfers between devices with their start and end apart: 21 -> 27, of which waited for: 20 -> 22; matrix products, arithmetic and copies ran while one was open for 11% -> 12% of each run, Pallas kernels for 0% -> 0%
where the time goes in v1:
time: 1420 us; the launch traced here: 1410 us
  waiting for transfers between devices  1030 us (73%)
  matrix products  153 us (11%)
  blocking collectives  105 us (7%)
  other arithmetic  60 us (4%)
  local copies, waits for them, and re-layouts  34.4 us (2%)
  between operations  17.7 us (1%)
  starting transfers between devices  14.6 us (1%)
    psum x2, waiting for transfers between devices, tensor_sum(): return lax.psum(values, 'tensor')  170 us
    reduce_scatter x1, waiting for transfers between devices, on_device(): lax.psum_scatter(grad_up.astype(jnp.bfloat16), ('dp', 'ctx'), scatter_dim...  128 us
    reduce_scatter x1, waiting for transfers between devices, on_device(): lax.psum_scatter(grad_gate.astype(jnp.bfloat16), ('dp', 'ctx'), scatter_d...  127 us
    reduce_scatter x1, waiting for transfers between devices, on_device(): lax.psum_scatter(grad_down.astype(jnp.bfloat16), ('dp', 'ctx'), scatter_d...  108 us
    psum x1, waiting for transfers between devices, on_device(): lax.psum(partial_value.astype(jnp.bfloat16), 'tensor').astype(jnp.float32)  70.6 us
    ppermute x3, waiting for transfers between devices, gather_around(): upper.append(lax.ppermute(upper[-1] if upper else value, axis, back))  57.4 us
    all_gather x1, waiting for transfers between devices, on_device(): lax.all_gather(w_down, ('dp', 'ctx'), axis=1, tiled=True)  52.3 us
    ppermute x4, waiting for transfers between devices, gather_around(): lower.append(lax.ppermute(lower[-1] if lower else value, axis, pairs))  50.6 us
  transfers between devices with their start and end apart: 27, of which 22 were waited for; matrix products, arithmetic and copies ran while one was open for 12% of the time, Pallas kernels for 0%

profile of v1, /device:TPU:0, one launch (start us, length us, event | category | flops | bytes accessed | tf_op | source)
XLA Modules:
  0.0 1413.9 jit_solution(9243245424056611303)
XLA Ops:
  9.4 17.9 %all-gather = bf16[8,1,256]{2,1,0:T(2,128)(2,1)S(1)} all-gather(bf16[1,1,256]{2,1,0:T(2,128)(2,1)S(1)} %reshape.304), channel_id=1, replica_groups=mesh['dp'=2,'ctx'=4,'tensor'=4] {'dp','ctx'}, dimensions={0}, use_global_device_ids=true | all-gather | bytes 4608 | tf_op jit(solution)/shard_map/all_gather | solution.py:137
  29.6 4.9 all-gather.11.cloned.1.call-done
  40.3 16.3 %all-reduce.8 = (bf16[128]{0:T(256)(128)(2,1)S(1)}, bf16[128]{0:T(256)(128)(2,1)S(1)}) all-reduce(bf16[128]{0:T(256)(128)(2,1)S(1)} %dynamic-update-slice, bf16[128]{0:T(256)(128)(2,1)S(1)} %dynamic-update-slice.1), channel_id=1, replica_groups=mesh['dp'=2,'ctx'=4,'tensor'=4] {'dp','ctx'}, use_global_device_ids=true, to_apply=%add | all-reduce | flops 256 | bytes 1024
  70.3 17.5 %all-gather.13.cloned.1.call-done = bf16[2048,256]{1,0:T(8,128)(2,1)} async-done(((bf16[512,256]{1,0:T(8,128)(2,1)}), bf16[2048,256]{1,0:T(8,128)(2,1)}) %all-gather.13.cloned.1.call-update) | async-done | bytes 1048592 | tf_op jit(solution)/shard_map/all_gather | solution.py:190
  90.2 27.7 %all-gather.19.cloned.1.call-done = bf16[2048,512]{1,0:T(8,128)(2,1)} async-done(((bf16[256,512]{1,0:T(8,128)(2,1)}), bf16[2048,512]{1,0:T(8,128)(2,1)}) %all-gather.19.cloned.1.call-update) | async-done | bytes 2097168 | tf_op jit(solution)/shard_map/all_gather | solution.py:133
  122.8 24.5 %all-gather.17.cloned.1.call-done = bf16[2048,256]{0,1:T(8,128)(2,1)} async-done(((bf16[512,256]{0,1:T(8,128)(2,1)}), bf16[2048,256]{0,1:T(8,128)(2,1)}) %all-gather.17.cloned.1.call-update) | async-done | bytes 1048592 | tf_op jit(solution)/shard_map/all_gather | solution.py:189
  147.3 14.0 fusion.83
  161.2 7.6 fusion.32
  168.9 9.8 all-gather.21.cloned.1.call-done
  178.7 4.9 fusion.84
  188.5 18.0 %collective-permute-done = bf16[256,1536]{1,0:T(8,128)(2,1)S(1)} collective-permute-done((bf16[256,1536]{1,0:T(8,128)(2,1)S(1)}, bf16[256,1536]{1,0:T(8,128)(2,1)S(1)}, u32[]{:S(2)}, u32[]{:S(2)}) %collective-permute-start) | collective-permute-done | bytes 786464 | tf_op jit(solution)/shard_map/ppermute | solution.py:26
  210.0 17.8 %collective-permute-done.1 = bf16[256,1536]{1,0:T(8,128)(2,1)S(1)} collective-permute-done((bf16[256,1536]{1,0:T(8,128)(2,1)S(1)}, bf16[256,1536]{1,0:T(8,128)(2,1)S(1)}, u32[]{:S(2)}, u32[]{:S(2)}) %collective-permute-start.1) | collective-permute-done | bytes 786464 | tf_op jit(solution)/shard_map/ppermute | solution.py:26
  228.6 15.2 %collective-permute-done.4 = bf16[256,1536]{1,0:T(8,128)(2,1)} collective-permute-done((bf16[256,1536]{1,0:T(8,128)(2,1)S(1)}, bf16[256,1536]{1,0:T(8,128)(2,1)}, u32[]{:S(2)}, u32[]{:S(2)}) %collective-permute-start.4) | collective-permute-done | bytes 786464 | tf_op jit(solution)/shard_map/ppermute | solution.py:28
  246.8 14.9 %collective-permute-done.2 = bf16[256,1536]{1,0:T(8,128)(2,1)} collective-permute-done((bf16[256,1536]{1,0:T(8,128)(2,1)S(1)}, bf16[256,1536]{1,0:T(8,128)(2,1)}, u32[]{:S(2)}, u32[]{:S(2)}) %collective-permute-start.2) | collective-permute-done | bytes 786464 | tf_op jit(solution)/shard_map/ppermute | solution.py:26
  262.9 41.2 %all-gather.1 = bf16[8,1,256]{2,1,0:T(2,128)(2,1)S(1)} all-gather(bf16[1,1,256]{2,1,0:T(2,128)(2,1)S(1)} %reshape.306), channel_id=1, replica_groups=mesh['dp'=2,'ctx'=4,'tensor'=4] {'dp','ctx'}, dimensions={0}, use_global_device_ids=true | all-gather | bytes 4608 | tf_op jit(solution)/shard_map/all_gather | solution.py:145
  317.7 42.2 %collective-permute-done.6 = bf16[256,1536]{1,0:T(8,128)(2,1)S(1)} collective-permute-done((bf16[256,1536]{1,0:T(8,128)(2,1)}, bf16[256,1536]{1,0:T(8,128)(2,1)S(1)}, u32[]{:S(2)}, u32[]{:S(2)}) %collective-permute-start.6) | collective-permute-done | bytes 786464 | tf_op jit(solution)/shard_map/ppermute | solution.py:28
  360.8 6.4 gather_fusion
  373.9 8.8 fusion.85
  382.6 52.3 %all-gather.25.cloned.1.call-done = bf16[1536,2048]{1,0:T(8,128)(2,1)} async-done(((bf16[1536,256]{1,0:T(8,128)(2,1)}), bf16[1536,2048]{1,0:T(8,128)(2,1)}) %all-gather.25.cloned.1.call-update) | async-done | bytes 6291472 | tf_op jit(solution)/shard_map/all_gather | solution.py:144
  434.9 6.4 fusion.87
  441.4 8.5 multiply_convert_fusion.2
  453.4 5.0 convolution_add_fusion
  458.4 4.9 fusion.86
  463.6 170.2 %all-reduce.18.cloned.1.call-done = (f32[512,2048]{1,0:T(8,128)}, f32[512,2048]{1,0:T(8,128)}) async-done(((f32[512,2048]{1,0:T(8,128)}, f32[512,2048]{1,0:T(8,128)}), (f32[512,2048]{1,0:T(8,128)}, f32[512,2048]{1,0:T(8,128)})) %all-reduce.18.cloned.1.call-update) | async-done | bytes 8388624 | tf_op jit(solution)/shard_map/psum | solution.py:88
  633.8 4.7 multiply_reduce_fusion
  638.5 6.3 subtract_add_fusion
  649.5 9.5 fusion.1
  658.9 11.6 fusion.3
  670.5 3.9 fusion.27
  674.6 10.0 fusion.20
  684.9 5.1 fusion.31
  694.1 4.8 convolution_convert_fusion.3
  699.0 8.2 convolution_convert_fusion.2
  707.3 8.2 convolution_convert_fusion.1
  723.4 40.6 %reduce-scatter.12.cloned.1.call-done = f32[512,256]{0,1:T(8,128)} async-done(((f32[2048,256]{0,1:T(8,128)}), f32[512,256]{0,1:T(8,128)}) %reduce-scatter.12.cloned.1.call-update) | async-done | bytes 524304 | tf_op jit(solution)/shard_map/reduce_scatter | solution.py:262
  766.7 4.4 add_convert_fusion
  771.1 8.2 convolution_convert_fusion
  784.8 29.8 %reduce-scatter.14.cloned.1.call-done = bf16[256,512]{1,0:T(8,128)(2,1)} async-done(((bf16[2048,512]{1,0:T(8,128)(2,1)}), bf16[256,512]{1,0:T(8,128)(2,1)}) %reduce-scatter.14.cloned.1.call-update) | async-done | bytes 262160 | tf_op jit(solution)/shard_map/reduce_scatter | solution.py:313
  816.4 48.6 %reduce-scatter.20.cloned.1.call-done = bf16[512,256]{1,0:T(8,128)(2,1)} async-done(((bf16[512,2048]{1,0:T(8,128)(2,1)}), bf16[512,256]{1,0:T(8,128)(2,1)}) %reduce-scatter.20.cloned.1.call-update) | async-done | bytes 262160 | tf_op jit(solution)/shard_map/reduce_scatter | solution.py:322
  866.8 127.4 %reduce-scatter.22.cloned.1.call-done = bf16[256,1536]{1,0:T(8,128)(2,1)} async-done(((bf16[2048,1536]{1,0:T(8,128)(2,1)}), bf16[256,1536]{1,0:T(8,128)(2,1)}) %reduce-scatter.22.cloned.1.call-update) | async-done | bytes 786448 | tf_op jit(solution)/shard_map/reduce_scatter | solution.py:325
  996.7 128.1 %reduce-scatter.24.cloned.1.call-done = bf16[256,1536]{1,0:T(8,128)(2,1)} async-done(((bf16[2048,1536]{1,0:T(8,128)(2,1)}), bf16[256,1536]{1,0:T(8,128)(2,1)}) %reduce-scatter.24.cloned.1.call-update) | async-done | bytes 786448 | tf_op jit(solution)/shard_map/reduce_scatter | solution.py:328
  1127.2 70.6 %all-reduce.16.cloned.1.call-done = bf16[512,2048]{1,0:T(8,128)(2,1)} async-done(((bf16[512,2048]{1,0:T(8,128)(2,1)}), bf16[512,2048]{1,0:T(8,128)(2,1)}) %all-reduce.16.cloned.1.call-update) | async-done | bytes 2097168 | tf_op jit(solution)/shard_map/psum | solution.py:293
  1201.0 20.0 %all-reduce.7 = (bf16[2048]{0:T(1024)(128)(2,1)S(1)}, bf16[2048]{0:T(1024)(128)(2,1)S(1)}, bf16[128]{0:T(256)(128)(2,1)S(1)}, bf16[128]{0:T(256)(128)(2,1)S(1)}) all-reduce(bf16[2048]{0:T(1024)(128)(2,1)S(1)} %get-tuple-element.15, ...), channel_id=11, replica_groups=mesh['dp'=2,'ctx'=4,'tensor'=4] {'dp','ctx'}, use_global_device_ids=true, to_apply=%region_27.28.clone | all-reduce | flops 4352 | bytes 17408
  1221.1 108.0 %reduce-scatter.26.cloned.1.call-done = bf16[1536,256]{1,0:T(8,128)(2,1)} async-done(((bf16[1536,2048]{1,0:T(8,128)(2,1)}), bf16[1536,256]{1,0:T(8,128)(2,1)}) %reduce-scatter.26.cloned.1.call-update) | async-done | bytes 786448 | tf_op jit(solution)/shard_map/reduce_scatter | solution.py:331
  1331.5 9.8 all-reduce.9
  1342.3 25.6 %reduce-scatter.16.cloned.1.call-done = bf16[256,256]{1,0:T(8,128)(2,1)} async-done(((bf16[2048,256]{1,0:T(8,128)(2,1)}), bf16[256,256]{1,0:T(8,128)(2,1)}) %reduce-scatter.16.cloned.1.call-update) | async-done | bytes 131088 | tf_op jit(solution)/shard_map/reduce_scatter | solution.py:316
  1370.1 6.3 fusion.15
  1376.5 28.6 %reduce-scatter.18.cloned.1.call-done = bf16[256,256]{1,0:T(8,128)(2,1)} async-done(((bf16[2048,256]{1,0:T(8,128)(2,1)}), bf16[256,256]{1,0:T(8,128)(2,1)}) %reduce-scatter.18.cloned.1.call-update) | async-done | bytes 131088 | tf_op jit(solution)/shard_map/reduce_scatter | solution.py:319
  (270 shorter events, 111.3 us)
Async XLA Ops:
  7.2 27.4 %all-gather.11.cloned.1.call-start = ((), (), s32[]{:S(2)}) async-start(), calls=%async_computation.9 | async-start | bytes 1179648 | tf_op jit(solution)/shard_map/all_gather | solution.py:135
  7.9 51.2 %all-gather.15.cloned.1.call-start = ((), (), s32[]{:S(2)}) async-start(), calls=%async_computation.11 | async-start | bytes 1179648 | tf_op jit(solution)/shard_map/all_gather | solution.py:134
  8.7 79.2 %all-gather.13.cloned.1.call-start = ((), (), s32[]{:S(2)}) async-start(), calls=%async_computation.10 | async-start | bytes 1310720 | tf_op jit(solution)/shard_map/all_gather | solution.py:190
  27.3 90.6 %copy-start.26 = (f32[8,1,256]{2,1,0:T(1,128)}, f32[8,1,256]{2,1,0:T(1,128)S(1)}, u32[]{:S(2)}) copy-start(f32[8,1,256]{2,1,0:T(1,128)S(1)} %convert_element_type.255) | copy-start | bytes 24580
  27.3 11.3 copy-start.38
  27.3 12.5 copy-start.40
  27.3 12.8 copy-start.41
  27.3 29.3 %copy-start.39 = (s32[1,13]{1,0:T(1,128)S(1)}, s32[1,13]{1,0:T(1,128)}, u32[]{:S(2)}) copy-start(s32[1,13]{1,0:T(1,128)} %param.16) | copy-start | bytes 160
  27.3 29.5 %copy-start.42 = (s32[1,13]{1,0:T(1,128)S(1)}, s32[1,13]{1,0:T(1,128)}, u32[]{:S(2)}) copy-start(s32[1,13]{1,0:T(1,128)} %param.17) | copy-start | bytes 160
  27.4 31.8 %copy-start.3 = (bf16[512,2048]{1,0:T(8,128)(2,1)S(1)}, bf16[512,2048]{1,0:T(8,128)(2,1)}, u32[]{:S(2)}) copy-start(bf16[512,2048]{1,0:T(8,128)(2,1)} %param.15) | copy-start | bytes 6291460
  29.6 88.3 %copy-start.32 = (f32[512]{0:T(512)}, f32[512]{0:T(512)S(1)}, u32[]{:S(2)}) copy-start(f32[512]{0:T(512)S(1)} %add_rsqrt_fusion.3) | copy-start | bytes 6148
  37.9 80.0 %all-gather.19.cloned.1.call-start = ((), (), s32[]{:S(2)}) async-start(), calls=%async_computation.13 | async-start | bytes 2359296 | tf_op jit(solution)/shard_map/all_gather | solution.py:133
  38.5 108.8 %all-gather.17.cloned.1.call-start = ((), (), s32[]{:S(2)}) async-start(), calls=%async_computation.12 | async-start | bytes 1310720 | tf_op jit(solution)/shard_map/all_gather | solution.py:189
  59.1 62.9 %copy-start.10 = (f32[512,64]{0,1:T(8,128)}, f32[512,64]{0,1:T(8,128)S(1)}, u32[]{:S(2)}) copy-start(f32[512,64]{0,1:T(8,128)S(1)} %get-tuple-element.50) | copy-start | bytes 393220
  59.1 62.9 %copy-start.12 = (f32[512,64]{0,1:T(8,128)}, f32[512,64]{0,1:T(8,128)S(1)}, u32[]{:S(2)}) copy-start(f32[512,64]{0,1:T(8,128)S(1)} %get-tuple-element.51) | copy-start | bytes 393220
  63.1 115.6 %all-gather.21.cloned.1.call-start = ((), (), s32[]{:S(2)}) async-start(), calls=%async_computation.14 | async-start | bytes 2359296 | tf_op jit(solution)/shard_map/all_gather | solution.py:136
  63.7 303.5 %all-reduce.14.cloned.1.call-start = ((), (), s32[]{:S(2)}) async-start(), calls=%async_computation.15 | async-start | bytes 8388608 | tf_op jit(solution)/shard_map/psum | solution.py:88
  64.2 56.7 %copy-start.34 = (f32[128]{0:T(128)}, f32[128]{0:T(128)S(1)}, u32[]{:S(2)}) copy-start(f32[128]{0:T(128)S(1)} %convert_element_type.203) | copy-start | bytes 1540
  122.8 38.4 %copy-start.15 = (bf16[512,4,64]{2,0,1:T(8,128)(2,1)}, bf16[512,4,64]{2,0,1:T(8,128)(2,1)S(1)}, u32[]{:S(2)}) copy-start(bf16[512,4,64]{2,0,1:T(8,128)(2,1)S(1)} %copy.66) | copy-start | bytes 786436
  183.6 79.2 %copy-start.43 = (bf16[256]{0:T(256)(128)(2,1)S(1)}, bf16[256]{0:T(256)(128)(2,1)}, u32[]{:S(2)}) copy-start(bf16[256]{0:T(256)(128)(2,1)} %param.26) | copy-start | bytes 1540
  183.7 190.2 %all-gather.23.cloned.1.call-start = ((), (), s32[]{:S(2)}) async-start(), calls=%async_computation.16 | async-start | bytes 7077888 | tf_op jit(solution)/shard_map/all_gather | solution.py:143
  184.4 250.5 %all-gather.25.cloned.1.call-start = ((), (), s32[]{:S(2)}) async-start(), calls=%async_computation.17 | async-start | bytes 7077888 | tf_op jit(solution)/shard_map/all_gather | solution.py:144
  185.1 448.6 %all-reduce.18.cloned.1.call-start = ((), (), s32[]{:S(2)}) async-start(), calls=%async_computation.28 | async-start | bytes 16777216 | tf_op jit(solution)/shard_map/psum | solution.py:88
  185.2 21.3 %collective-permute-start = (bf16[256,1536]{1,0:T(8,128)(2,1)S(1)}, bf16[256,1536]{1,0:T(8,128)(2,1)S(1)}, u32[]{:S(2)}, u32[]{:S(2)}) collective-permute-start(bf16[256,1536]{1,0:T(8,128)(2,1)S(1)} %copy-done.19), channel_id=1, source_target_pairs={{0,4},{4,8},{8,12},{12,16},{16,20},{20,24},{24,28},{28,0},{1,5},{5... | collective-permute-start | bytes 2359304 | tf_op jit(solution)/shard_map/ppermute | solution.py:26
  206.5 37.3 %copy-start.20 = (bf16[256,1536]{1,0:T(8,128)(2,1)}, bf16[256,1536]{1,0:T(8,128)(2,1)S(1)}, u32[]{:S(2)}) copy-start(bf16[256,1536]{1,0:T(8,128)(2,1)S(1)} %collective-permute-done) | copy-start | bytes 2359300
  206.5 21.3 %collective-permute-start.1 = (bf16[256,1536]{1,0:T(8,128)(2,1)S(1)}, bf16[256,1536]{1,0:T(8,128)(2,1)S(1)}, u32[]{:S(2)}, u32[]{:S(2)}) collective-permute-start(bf16[256,1536]{1,0:T(8,128)(2,1)S(1)} %collective-permute-done), channel_id=1, source_target_pairs={{0,4},{4,8},{8,12},{12,16},{16,20},{20,24},{24,28},{28,0},{1,5},{5... | collective-permute-start | bytes 2359304 | tf_op jit(solution)/shard_map/ppermute | solution.py:26
  208.2 35.6 %collective-permute-start.4 = (bf16[256,1536]{1,0:T(8,128)(2,1)S(1)}, bf16[256,1536]{1,0:T(8,128)(2,1)}, u32[]{:S(2)}, u32[]{:S(2)}) collective-permute-start(bf16[256,1536]{1,0:T(8,128)(2,1)S(1)} %copy-done.19), channel_id=1, source_target_pairs={{4,0},{8,4},{12,8},{16,12},{20,16},{24,20},{28,24},{0,28},{5,1},{9... | collective-permute-start | bytes 2359304 | tf_op jit(solution)/shard_map/ppermute | solution.py:28
  227.8 19.0 %copy-start.22 = (bf16[256,1536]{1,0:T(8,128)(2,1)}, bf16[256,1536]{1,0:T(8,128)(2,1)S(1)}, u32[]{:S(2)}) copy-start(bf16[256,1536]{1,0:T(8,128)(2,1)S(1)} %collective-permute-done.1) | copy-start | bytes 2359300
  227.8 33.9 %collective-permute-start.2 = (bf16[256,1536]{1,0:T(8,128)(2,1)S(1)}, bf16[256,1536]{1,0:T(8,128)(2,1)}, u32[]{:S(2)}, u32[]{:S(2)}) collective-permute-start(bf16[256,1536]{1,0:T(8,128)(2,1)S(1)} %collective-permute-done.1), channel_id=1, source_target_pairs={{0,4},{4,8},{8,12},{12,16},{16,20},{20,24},{24,28},{28,0},{1,5},{5... | collective-permute-start | bytes 2359304 | tf_op jit(solution)/shard_map/ppermute | solution.py:26
  243.8 60.3 %collective-permute-start.5 = (bf16[256,1536]{1,0:T(8,128)(2,1)}, bf16[256,1536]{1,0:T(8,128)(2,1)}, u32[]{:S(2)}, u32[]{:S(2)}) collective-permute-start(bf16[256,1536]{1,0:T(8,128)(2,1)} %collective-permute-done.4), channel_id=1, source_target_pairs={{4,0},{8,4},{12,8},{16,12},{20,16},{24,20},{28,24},{0,28},{5,1},{9... | collective-permute-start | bytes 2359304 | tf_op jit(solution)/shard_map/ppermute | solution.py:28
  261.7 43.7 %collective-permute-start.3 = (bf16[256,1536]{1,0:T(8,128)(2,1)}, bf16[256,1536]{1,0:T(8,128)(2,1)}, u32[]{:S(2)}, u32[]{:S(2)}) collective-permute-start(bf16[256,1536]{1,0:T(8,128)(2,1)} %collective-permute-done.2), channel_id=1, source_target_pairs={{0,4},{4,8},{8,12},{12,16},{16,20},{20,24},{24,28},{28,0},{1,5},{5... | collective-permute-start | bytes 2359304 | tf_op jit(solution)/shard_map/ppermute | solution.py:26
  304.1 55.8 %collective-permute-start.6 = (bf16[256,1536]{1,0:T(8,128)(2,1)}, bf16[256,1536]{1,0:T(8,128)(2,1)S(1)}, u32[]{:S(2)}, u32[]{:S(2)}) collective-permute-start(bf16[256,1536]{1,0:T(8,128)(2,1)} %collective-permute-done.5), channel_id=1, source_target_pairs={{4,0},{8,4},{12,8},{16,12},{20,16},{24,20},{28,24},{0,28},{5,1},{9... | collective-permute-start | bytes 2359304 | tf_op jit(solution)/shard_map/ppermute | solution.py:28
  434.9 15.0 %slice-start.6 = ((s8[6291456]{0:T(1024)(128)(4,1)}), s8[4194304]{0:T(1024)(128)(4,1)S(1)}, s32[]{:S(2)}) async-start(s8[6291456]{0:T(1024)(128)(4,1)} %bitcast.269), calls=%async_computation.35 | async-start | bytes 8388608
  434.9 18.4 %slice-start.4 = ((s8[6291456]{0:T(1024)(128)(4,1)}), s8[4194304]{0:T(1024)(128)(4,1)S(1)}, s32[]{:S(2)}) async-start(s8[6291456]{0:T(1024)(128)(4,1)} %bitcast.239), calls=%async_computation.33 | async-start | bytes 8388608
  441.4 12.0 slice-start.5
  441.4 17.1 %slice-start.8 = ((s8[6291456]{0:T(1024)(128)(4,1)}), s8[4194304]{0:T(1024)(128)(4,1)S(1)}, s32[]{:S(2)}) async-start(s8[6291456]{0:T(1024)(128)(4,1)} %bitcast.271), calls=%async_computation.37 | async-start | bytes 8388608
  463.4 255.6 %reduce-scatter.10.cloned.1.call-start = ((), (), s32[]{:S(2)}) async-start(), calls=%async_computation.18 | async-start | bytes 2621440 | tf_op jit(solution)/shard_map/reduce_scatter | solution.py:256
  633.8 15.3 %slice-start = ((s8[16777216]{0:T(1024)(128)(4,1)}), s8[4194304]{0:T(1024)(128)(4,1)S(1)}, s32[]{:S(2)}) async-start(s8[16777216]{0:T(1024)(128)(4,1)} %bitcast.235), calls=%async_computation.29 | async-start | bytes 8388608
  658.9 11.6 copy-start.16
  674.5 89.5 %reduce-scatter.12.cloned.1.call-start = ((), (), s32[]{:S(2)}) async-start(), calls=%async_computation.19 | async-start | bytes 2621440 | tf_op jit(solution)/shard_map/reduce_scatter | solution.py:262
  684.6 130.0 %reduce-scatter.14.cloned.1.call-start = ((), (), s32[]{:S(2)}) async-start(), calls=%async_computation.21 | async-start | bytes 2359296 | tf_op jit(solution)/shard_map/reduce_scatter | solution.py:313
  694.1 171.0 %reduce-scatter.20.cloned.1.call-start = ((), (), s32[]{:S(2)}) async-start(), calls=%async_computation.24 | async-start | bytes 2359296 | tf_op jit(solution)/shard_map/reduce_scatter | solution.py:322
  699.0 295.2 %reduce-scatter.22.cloned.1.call-start = ((), (), s32[]{:S(2)}) async-start(), calls=%async_computation.25 | async-start | bytes 7077888 | tf_op jit(solution)/shard_map/reduce_scatter | solution.py:325
  707.3 417.5 %reduce-scatter.24.cloned.1.call-start = ((), (), s32[]{:S(2)}) async-start(), calls=%async_computation.26 | async-start | bytes 7077888 | tf_op jit(solution)/shard_map/reduce_scatter | solution.py:328
  715.5 482.3 %all-reduce.16.cloned.1.call-start = ((), (), s32[]{:S(2)}) async-start(), calls=%async_computation.20 | async-start | bytes 4194304 | tf_op jit(solution)/shard_map/psum | solution.py:293
  771.0 558.1 %reduce-scatter.26.cloned.1.call-start = ((), (), s32[]{:S(2)}) async-start(), calls=%async_computation.27 | async-start | bytes 7077888 | tf_op jit(solution)/shard_map/reduce_scatter | solution.py:331
  779.3 588.5 %reduce-scatter.16.cloned.1.call-start = ((), (), s32[]{:S(2)}) async-start(), calls=%async_computation.22 | async-start | bytes 1179648 | tf_op jit(solution)/shard_map/reduce_scatter | solution.py:316
  781.4 623.7 %reduce-scatter.18.cloned.1.call-start = ((), (), s32[]{:S(2)}) async-start(), calls=%async_computation.23 | async-start | bytes 1179648 | tf_op jit(solution)/shard_map/reduce_scatter | solution.py:319
  (38 other events, 178.9 us)
Sparse Core Ops, SparseCore 0:
  9.6 24.9 all-gather.10
  36.2 22.2 all-gather.14
  60.6 27.1 all-gather.12
  89.3 28.5 all-gather.18
  119.9 27.3 all-gather.16
  148.7 29.9 all-gather.20
  183.8 102.6 all-reduce.13
  288.0 81.1 all-gather.22
  370.9 63.9 all-gather.24
  463.5 170.2 all-reduce.17
  674.6 44.3 reduce-scatter.9
  721.1 42.8 reduce-scatter.11
  766.3 48.2 reduce-scatter.13
  816.7 48.2 reduce-scatter.19
  867.2 126.9 reduce-scatter.21
  996.4 128.3 reduce-scatter.23
  1127.7 70.0 all-reduce.15
  1200.0 129.0 reduce-scatter.25
  1331.4 36.4 reduce-scatter.15
  1370.0 35.0 reduce-scatter.17
